TPU v7x, 32 devices: a whole 2x2x4 slice. The times are simulated.
32 devices in a mesh: lat: 4 (over y, x), lon: 8 (over z, core).
Axes of the slice: x: 2, y: 2, z: 4, core: 2. Of those that a mesh axis runs over, the one named last changes fastest.
Arguments:
- grid_state: float32 [48, 120, 384], P('lat', 'lon'), may hold values from -6 to 6
- norm_gain: float32 [2, 384], replicated, may hold values from 0.25 to 1.75
- conv_weight: bfloat16 [2, 3, 3, 384, 384], replicated, may hold values from -0.109375 to 0.109375
- filter_weight: bfloat16 [48, 384, 384], P('lat'), may hold values from -0.3125 to 0.3125
- degree_keep: int32 [48, 48], P('lat', 'lon'), may hold values 0 or 1
Outputs:
- updated: float32 [48, 120, 384], P('lat', 'lon')
Inputs may be any that keep to these rules, and one draw needn't show every extreme that they name: degree_keep[l, m] is 0 or 1 for degree l and order m.
All inputs are finite; a program needn't handle non-finite values. No bound on the sum of `degree_keep` on one device may be relied on, other than what follows from the above.
Results may differ from a plain program's by a relative error of at most 0.008.
Values may be sent and summed in bfloat16 or wider, within the bound.
A program may use at most 64 MiB of HBM per device.

v0:
```python
import math
import jax
import jax.numpy as jnp
from jax import lax
from jax.sharding import PartitionSpec as P

epsilon = 1e-06


def extended(array, sides, width):
    for axis, dim in sides:
        size, length = (lax.axis_size(axis), array.shape[dim])
        up = [(i, (i + 1) % size) for i in range(size)]
        down = [(j, i) for i, j in up]
        last = lax.slice_in_dim(array, length - width, length, axis=dim)
        first = lax.slice_in_dim(array, 0, width, axis=dim)
        before = lax.ppermute(last, axis, up)
        after = lax.ppermute(first, axis, down)
        array = jnp.concatenate([before, array, after], axis=dim)
    return array


def colatitude(row_index, total_rows, float_type):
    theta_rows = (row_index.astype(float_type) + 0.5) * (math.pi / total_rows)
    return (jnp.cos(theta_rows), jnp.sin(theta_rows))


def legendre_table(orders, cosine, sine_values, amount):
    float_type = cosine.dtype
    order_f = orders.astype(float_type)[:, None]
    order_i = orders[:, None]
    column = cosine[None, :]
    log_start = (
        0.5
        * (
            jnp.log((2.0 * order_f + 1.0) / (4.0 * math.pi))
            + jax.scipy.special.gammaln(order_f + 0.5)
            - jax.scipy.special.gammaln(order_f + 1.0)
            - 0.5 * math.log(math.pi)
        )
        + order_f * jnp.log(sine_values)[None, :]
    )
    sectoral = jnp.exp(log_start)

    def advance(carry, degree):
        before, latest = carry
        degree_f = degree.astype(float_type)
        growth = jnp.sqrt(
            jnp.maximum(4.0 * degree_f * degree_f - 1.0, 1.0)
            / jnp.maximum(degree_f * degree_f - order_f * order_f, 1.0)
        )
        prior = degree_f - 1.0
        damping = jnp.sqrt(
            jnp.maximum(prior * prior - order_f * order_f, 0.0)
            / jnp.maximum(4.0 * prior * prior - 1.0, 1.0)
        )
        grown = growth * (column * latest - damping * before)
        fresh = jnp.where(
            degree < order_i, jnp.zeros_like(grown), jnp.where(degree == order_i, sectoral, grown)
        )
        return ((latest, fresh), fresh)

    zero_rows = jnp.zeros((orders.shape[0], cosine.shape[0]), float_type)
    _, assoc_basis = lax.scan(
        advance, (zero_rows, zero_rows), jnp.arange(amount, dtype=jnp.int32), unroll=16
    )
    return assoc_basis


def forward_table(columns, modes, total_cols, float_type):
    lon_index = columns[:, None]
    order_index = jnp.arange(modes, dtype=jnp.int32)[None, :]
    phase = (lon_index * order_index % total_cols).astype(float_type) * (2.0 * math.pi / total_cols)
    factor = 2.0 * math.pi / total_cols
    return jnp.stack([jnp.cos(phase) * factor, -jnp.sin(phase) * factor], axis=2).reshape(
        columns.shape[0], 2 * modes
    )


def inverse_table(modes, total_cols, float_type):
    order_index = jnp.arange(modes, dtype=jnp.int32)[:, None]
    lon_index = jnp.arange(total_cols, dtype=jnp.int32)[None, :]
    phase = (lon_index * order_index % total_cols).astype(float_type) * (2.0 * math.pi / total_cols)
    factor = jnp.where(order_index == 0, 1.0, 2.0).astype(float_type)
    return jnp.stack([jnp.cos(phase) * factor, -jnp.sin(phase) * factor], axis=1).reshape(
        2 * modes, total_cols
    )


def paired(form, data, table):
    upper_part = table.astype(jnp.bfloat16)
    lower_part = (table - upper_part.astype(jnp.float32)).astype(jnp.bfloat16)
    first = jnp.einsum(form, data, upper_part, preferred_element_type=jnp.float32)
    return first + jnp.einsum(form, data, lower_part, preferred_element_type=jnp.float32)


def to_columns(values):
    return lax.all_to_all(values, "lon", split_axis=2, concat_axis=0, tiled=True)


def to_channels(values):
    return lax.all_to_all(values, "lon", split_axis=0, concat_axis=2, tiled=True)


def grid_rims(normed):
    padded = extended(normed, (("lat", 0), ("lon", 1)), 1)
    place = lax.axis_index("lat")
    final_place = lax.axis_size("lat") - 1
    zero_line = jnp.zeros_like(padded[:1])
    upper_rim = jnp.where(place == 0, zero_line, padded[:1])
    lower_rim = jnp.where(place == final_place, zero_line, padded[-1:])
    return jnp.concatenate([upper_rim, padded[1:-1], lower_rim], axis=0)


def conv_taps(padded, weight, row_count, col_count):
    channels = padded.shape[2]
    running = jnp.zeros((row_count * col_count, weight.shape[3]), jnp.float32)
    for row_tap in range(3):
        for col_tap in range(3):
            window = padded[row_tap : row_tap + row_count, col_tap : col_tap + col_count].reshape(
                row_count * col_count, channels
            )
            running = running + jnp.dot(
                window, weight[row_tap, col_tap], preferred_element_type=jnp.float32
            )
    return running.reshape(row_count, col_count, weight.shape[3])


def conv_block(grid_state, gain, weight):
    row_count, col_count, channels = grid_state.shape
    scale_rows = lax.rsqrt(jnp.mean(grid_state * grid_state, axis=-1, keepdims=True) + epsilon)
    normed = (grid_state * scale_rows * gain).astype(jnp.bfloat16)
    padded = grid_rims(normed)
    mixture = conv_taps(padded, weight, row_count, col_count)
    return grid_state + jax.nn.gelu(mixture, approximate=False)


def per_device(grid_state, norm_gain, conv_weight, filter_weight, degree_keep):
    f32 = jnp.float32
    for depth_index in range(2):
        grid_state = conv_block(grid_state, norm_gain[depth_index], conv_weight[depth_index])
    row_count, col_count, channels = grid_state.shape
    lat_parts = lax.axis_size("lat")
    lon_parts = lax.axis_size("lon")
    total_rows = row_count * lat_parts
    total_cols = col_count * lon_parts
    local_modes = total_rows // lon_parts
    share = channels // lon_parts
    columns = to_columns(jnp.transpose(grid_state.astype(jnp.bfloat16), (1, 0, 2)))
    flat_columns = columns.reshape(total_cols, row_count * share)
    dft_table = forward_table(jnp.arange(total_cols), total_rows, total_cols, f32)
    spectrum = paired("lx,lk->kx", flat_columns, dft_table).astype(jnp.bfloat16)
    spectrum = to_channels(spectrum.reshape(2 * total_rows, row_count, share))
    spectrum = jnp.transpose(spectrum, (1, 0, 2)).reshape(row_count, local_modes, 2 * channels)
    orders = lax.axis_index("lon") * local_modes + jnp.arange(local_modes, dtype=jnp.int32)
    keep_mask = degree_keep.astype(f32)
    cosine, sine_values = colatitude(jnp.arange(total_rows), total_rows, f32)
    assoc_basis = legendre_table(orders, cosine, sine_values, total_rows)
    weighted = assoc_basis * (sine_values * (math.pi / total_rows))[None, None, :]
    first_here = lax.axis_index("lat") * row_count
    own_weighted = lax.dynamic_slice_in_dim(weighted, first_here, row_count, 0)
    own_rows_basis = lax.dynamic_slice_in_dim(assoc_basis, first_here, row_count, 2)
    basis_rows = own_weighted
    coefficients = paired(
        "imx,lmi->lmx", lax.all_gather(spectrum, "lat", axis=0, tiled=True), basis_rows
    ).astype(jnp.bfloat16)
    flat_coeffs = coefficients.reshape(row_count, 2 * local_modes, channels)
    mixture = jnp.einsum("lkc,lcd->lkd", flat_coeffs, filter_weight, preferred_element_type=f32)
    mixture = mixture.reshape(row_count, local_modes, 2, channels) * keep_mask[:, :, None, None]
    filtered = mixture.reshape(row_count, local_modes, 2 * channels).astype(jnp.bfloat16)
    basis_rows = own_rows_basis
    synthesis = paired(
        "lmx,lmi->imx", lax.all_gather(filtered, "lat", axis=0, tiled=True), basis_rows
    ).astype(jnp.bfloat16)
    by_order = jnp.transpose(synthesis.reshape(row_count, 2 * local_modes, channels), (1, 0, 2))
    returned = to_columns(by_order)
    flat_returned = returned.reshape(2 * total_rows, row_count * share)
    physical = paired(
        "kx,kl->lx", flat_returned, inverse_table(total_rows, total_cols, f32)
    ).astype(jnp.bfloat16)
    physical = to_channels(physical.reshape(total_cols, row_count, share))
    physical = jnp.transpose(physical, (1, 0, 2))
    return grid_state + jax.nn.gelu(physical.astype(f32), approximate=False)


def solution(mesh):
    in_specs = (P("lat", "lon", None), P(), P(), P("lat", None, None), P("lat", "lon"))
    out_specs = P("lat", "lon", None)
    return jax.shard_map(
        per_device, mesh=mesh, in_specs=in_specs, out_specs=out_specs, check_vma=False
    )
```

profile of v0, /device:TPU:0, one launch (start us, length us, event | category | flops | bytes accessed | tf_op | source)
XLA Modules:
  0.0 426.2 jit_solution(8437420346642597354)
XLA Ops:
  4.9 3.0 collective-permute-start
  11.8 5.6 %slice_bitcast_fusion = (bf16[3,3,384,384]{3,2,1,0:T(8,128)(2,1)}, bf16[3,3,384,384]{3,2,1,0:T(8,128)(2,1)}) fusion(bf16[2,3,3,384,384]{4,3,2,1,0:T(8,128)(2,1)} %param.9), kind=kLoop, calls=%fused_computation.125 | loop fusion | bytes 10616832 | tf_op jit(solution)/shard_map/squeeze | solution.py:141
  17.4 152.1 %while.21 = (s32[]{:T(128)}, f32[6,48]{1,0:T(8,128)}, f32[6,48]{1,0:T(8,128)}, f32[3,16,6,48]{3,2,1,0:T(8,128)}, s32[3,16]{1,0:T(4,128)}, /*index=5*/s32[]{:T(12...) while((s32[]{:T(128)}, f32[6,48]{1,0:T(8,128)}, ...), condition=%wide.region_3.4_spmd.clone.clone.clone.clone, body=%wide.region_2.3_spmd.clone.clone.clone.clone.sunk | while | flops 65138 | bytes 363896 | solution.py:64
  174.8 3.5 collective-permute-start.3
  224.2 3.5 collective-permute-start.7
  264.1 2.5 convert_bitcast_fusion
  266.6 2.8 copy.96
  269.4 3.5 reshape.1588
  272.9 4.0 all-to-all-start
  283.8 3.5 reshape.1589
  287.3 3.4 copy.97
  301.3 4.3 %all-to-all-start.1 = ((bf16[8,2,3456]{2,1,0:T(2,128)(2,1)}), bf16[8,2,3456]{2,1,0:T(2,128)(2,1)}, u32[]{:S(2)}, u32[]{:S(2)}) async-start(bf16[8,2,3456]{2,1,0:T(2,128)(2,1)} %reshape.1590), calls=%async_computation.1 | async-start | bytes 221184 | tf_op jit(solution)/shard_map/all_to_all | solution.py:102
  306.4 5.8 %all-to-all-done.1 = bf16[8,2,3456]{2,1,0:T(2,128)(2,1)} async-done(((bf16[8,2,3456]{2,1,0:T(2,128)(2,1)}), bf16[8,2,3456]{2,1,0:T(2,128)(2,1)}, u32[]{:S(2)}, u32[]{:S(2)}) %all-to-all-start.1) | async-done | bytes 110624 | tf_op jit(solution)/shard_map/all_to_all | solution.py:102
  321.4 11.5 %all_gather.6 = bf16[48,6,768]{2,1,0:T(8,128)(2,1)S(1)} all-gather(bf16[12,6,768]{2,1,0:T(8,128)(2,1)} %reshape.1571), channel_id=1, replica_groups=mesh['lat'=4,'lon'=8] {'lat'}, dimensions={0}, use_global_device_ids=true | all-gather | bytes 552960 | tf_op jit(solution)/shard_map/all_gather | solution.py:165
  337.4 2.2 fusion.151
  342.4 10.4 %all_gather.7 = bf16[48,6,768]{2,1,0:T(8,128)(2,1)S(1)} all-gather(bf16[12,6,768]{2,1,0:T(8,128)(2,1)S(1)} %multiply_convert_fusion), channel_id=1, replica_groups=mesh['lat'=4,'lon'=8] {'lat'}, dimensions={0}, use_global_device_ids=true | all-gather | bytes 552960 | tf_op jit(solution)/shard_map/all_gather | solution.py:173
  357.2 2.8 copy.111
  360.0 3.4 reshape.1592
  363.4 4.0 all-to-all-start.2
  370.2 3.7 all-to-all-done.2
  373.9 3.4 reshape.1593
  377.3 3.2 copy.112
  389.8 10.8 %all_to_all.57 = bf16[8,2,4320]{2,1,0:T(2,128)(2,1)} all-to-all(bf16[8,2,4320]{2,1,0:T(2,128)(2,1)} %reshape.1594), channel_id=1, replica_groups=mesh['lat'=4,'lon'=8] {'lon'}, dimensions={0} | all-to-all | bytes 276480 | tf_op jit(solution)/shard_map/all_to_all | solution.py:102
  423.7 2.5 fusion.67
  (468 shorter events, 291.1 us)
Async XLA Ops:
  0.0 337.4 %copy-start = (bf16[12,384,384]{2,1,0:T(8,128)(2,1)S(1)}, bf16[12,384,384]{2,1,0:T(8,128)(2,1)}, u32[]{:S(2)}) copy-start(bf16[12,384,384]{2,1,0:T(8,128)(2,1)} %param.10) | copy-start | bytes 10616836
  4.9 168.3 %collective-permute-start = (bf16[1,15,384]{2,1,0:T(8,128)(2,1)}, bf16[1,15,384]{2,1,0:T(8,128)(2,1)}, u32[]{:S(2)}, u32[]{:S(2)}) collective-permute-start(bf16[1,15,384]{2,1,0:T(8,128)(2,1)} %get-tuple-element.566), channel_id=1, source_target_pairs={{0,8},{8,16},{16,24},{24,0},{1,9},{9,17},{17,25},{25,1},{2,10},{10... | collective-permute-start | bytes 34568 | tf_op jit(solution)/shard_map/ppermute | solution.py:17
  7.8 165.4 %collective-permute-start.1 = (bf16[1,15,384]{2,1,0:T(8,128)(2,1)}, bf16[1,15,384]{2,1,0:T(8,128)(2,1)}, u32[]{:S(2)}, u32[]{:S(2)}) collective-permute-start(bf16[1,15,384]{2,1,0:T(8,128)(2,1)} %get-tuple-element.567), channel_id=1, source_target_pairs={{8,0},{16,8},{24,16},{0,24},{9,1},{17,9},{25,17},{1,25},{10,2},{18... | collective-permute-start | bytes 34568 | tf_op jit(solution)/shard_map/ppermute | solution.py:18
  42.2 6.6 %copy-start.25 = (f32[6]{0:T(128)}, f32[6]{0:T(128)S(1)}, u32[]{:S(2)}) copy-start(f32[6]{0:T(128)S(1)} %get-tuple-element.771) | copy-start | bytes 76 | tf_op jit(solution)/shard_map/while
  50.2 4.5 %copy-start.6 = (f32[6,48]{1,0:T(8,128)}, f32[6,48]{1,0:T(8,128)S(1)}, u32[]{:S(2)}) copy-start(f32[6,48]{1,0:T(8,128)S(1)} %get-tuple-element.790) | copy-start | bytes 3460 | tf_op jit(solution)/shard_map/while
  92.9 6.6 %copy-start.25 = (f32[6]{0:T(128)}, f32[6]{0:T(128)S(1)}, u32[]{:S(2)}) copy-start(f32[6]{0:T(128)S(1)} %get-tuple-element.771) | copy-start | bytes 76 | tf_op jit(solution)/shard_map/while
  100.9 4.5 %copy-start.6 = (f32[6,48]{1,0:T(8,128)}, f32[6,48]{1,0:T(8,128)S(1)}, u32[]{:S(2)}) copy-start(f32[6,48]{1,0:T(8,128)S(1)} %get-tuple-element.790) | copy-start | bytes 3460 | tf_op jit(solution)/shard_map/while
  143.6 6.6 %copy-start.25 = (f32[6]{0:T(128)}, f32[6]{0:T(128)S(1)}, u32[]{:S(2)}) copy-start(f32[6]{0:T(128)S(1)} %get-tuple-element.771) | copy-start | bytes 76 | tf_op jit(solution)/shard_map/while
  151.6 4.5 %copy-start.6 = (f32[6,48]{1,0:T(8,128)}, f32[6,48]{1,0:T(8,128)S(1)}, u32[]{:S(2)}) copy-start(f32[6,48]{1,0:T(8,128)S(1)} %get-tuple-element.790) | copy-start | bytes 3460 | tf_op jit(solution)/shard_map/while
  174.8 5.3 %collective-permute-start.2 = (bf16[14,1,384]{2,1,0:T(2,128)(2,1)}, bf16[14,1,384]{2,1,0:T(2,128)(2,1)}, u32[]{:S(2)}, u32[]{:S(2)}) collective-permute-start(bf16[14,1,384]{2,1,0:T(2,128)(2,1)} %get-tuple-element.560), channel_id=1, source_target_pairs={{0,1},{1,2},{2,3},{3,4},{4,5},{5,6},{6,7},{7,0},{8,9},{9,10},{10,1... | collective-permute-start | bytes 32264 | tf_op jit(solution)/shard_map/ppermute | solution.py:17
  174.8 5.3 %collective-permute-start.3 = (bf16[14,1,384]{2,1,0:T(2,128)(2,1)}, bf16[14,1,384]{2,1,0:T(2,128)(2,1)}, u32[]{:S(2)}, u32[]{:S(2)}) collective-permute-start(bf16[14,1,384]{2,1,0:T(2,128)(2,1)} %get-tuple-element.561), channel_id=1, source_target_pairs={{1,0},{2,1},{3,2},{4,3},{5,4},{6,5},{7,6},{0,7},{9,8},{10,9},{11,1... | collective-permute-start | bytes 32264 | tf_op jit(solution)/shard_map/ppermute | solution.py:18
  201.9 5.4 %copy-start.13 = (bf16[180,384]{1,0:T(8,128)(2,1)S(1)}, bf16[180,384]{1,0:T(8,128)(2,1)}, u32[]{:S(2)}) copy-start(bf16[180,384]{1,0:T(8,128)(2,1)} %reshape.1554) | copy-start | bytes 414724
  201.9 6.6 %copy-start.9 = (bf16[180,384]{1,0:T(8,128)(2,1)S(1)}, bf16[180,384]{1,0:T(8,128)(2,1)}, u32[]{:S(2)}) copy-start(bf16[180,384]{1,0:T(8,128)(2,1)} %reshape.1555) | copy-start | bytes 414724
  206.1 9.8 %copy-start.38 = (f32[384]{0:T(512)S(1)}, f32[384]{0:T(512)}, u32[]{:S(2)}) copy-start(f32[384]{0:T(512)} %get-tuple-element.402) | copy-start | bytes 4612
  217.2 5.9 %collective-permute-start.4 = (bf16[1,15,384]{2,1,0:T(8,128)(2,1)}, bf16[1,15,384]{2,1,0:T(8,128)(2,1)S(1)}, u32[]{:S(2)}, u32[]{:S(2)}) collective-permute-start(bf16[1,15,384]{2,1,0:T(8,128)(2,1)} %get-tuple-element.564), channel_id=1, source_target_pairs={{0,8},{8,16},{16,24},{24,0},{1,9},{9,17},{17,25},{25,1},{2,10},{10... | collective-permute-start | bytes 34568 | tf_op jit(solution)/shard_map/ppermute | solution.py:17
  218.3 4.8 %collective-permute-start.5 = (bf16[1,15,384]{2,1,0:T(8,128)(2,1)}, bf16[1,15,384]{2,1,0:T(8,128)(2,1)}, u32[]{:S(2)}, u32[]{:S(2)}) collective-permute-start(bf16[1,15,384]{2,1,0:T(8,128)(2,1)} %get-tuple-element.565), channel_id=1, source_target_pairs={{8,0},{16,8},{24,16},{0,24},{9,1},{17,9},{25,17},{1,25},{10,2},{18... | collective-permute-start | bytes 34568 | tf_op jit(solution)/shard_map/ppermute | solution.py:18
  224.1 5.6 %collective-permute-start.6 = (bf16[14,1,384]{2,1,0:T(2,128)(2,1)S(1)}, bf16[14,1,384]{2,1,0:T(2,128)(2,1)S(1)}, u32[]{:S(2)}, u32[]{:S(2)}) collective-permute-start(bf16[14,1,384]{2,1,0:T(2,128)(2,1)S(1)} %get-tuple-element.556), channel_id=1, source_target_pairs={{0,1},{1,2},{2,3},{3,4},{4,5},{5,6},{6,7},{7,0},{8,9},{9,10},{10,1... | collective-permute-start | bytes 32264 | tf_op jit(solution)/shard_map/ppermute | solution.py:17
  224.2 5.5 %collective-permute-start.7 = (bf16[14,1,384]{2,1,0:T(2,128)(2,1)S(1)}, bf16[14,1,384]{2,1,0:T(2,128)(2,1)S(1)}, u32[]{:S(2)}, u32[]{:S(2)}) collective-permute-start(bf16[14,1,384]{2,1,0:T(2,128)(2,1)S(1)} %get-tuple-element.557), channel_id=1, source_target_pairs={{1,0},{2,1},{3,2},{4,3},{5,4},{6,5},{7,6},{0,7},{9,8},{10,9},{11,1... | collective-permute-start | bytes 32264 | tf_op jit(solution)/shard_map/ppermute | solution.py:18
  252.0 5.4 %copy-start.14 = (bf16[180,384]{1,0:T(8,128)(2,1)S(1)}, bf16[180,384]{1,0:T(8,128)(2,1)}, u32[]{:S(2)}) copy-start(bf16[180,384]{1,0:T(8,128)(2,1)} %reshape.1563) | copy-start | bytes 414724
  252.0 6.6 %copy-start.10 = (bf16[180,384]{1,0:T(8,128)(2,1)S(1)}, bf16[180,384]{1,0:T(8,128)(2,1)}, u32[]{:S(2)}) copy-start(bf16[180,384]{1,0:T(8,128)(2,1)} %reshape.1564) | copy-start | bytes 414724
  264.1 17.1 %copy-start.39 = (s32[12,6]{0,1:T(8,128)S(1)}, s32[12,6]{0,1:T(8,128)}, u32[]{:S(2)}) copy-start(s32[12,6]{0,1:T(8,128)} %param.11) | copy-start | bytes 868
  272.9 10.9 %all-to-all-start = ((bf16[8,2,4320]{2,1,0:T(2,128)(2,1)}), bf16[8,2,4320]{2,1,0:T(2,128)(2,1)}, u32[]{:S(2)}, u32[]{:S(2)}) async-start(bf16[8,2,4320]{2,1,0:T(2,128)(2,1)} %reshape.1588), calls=%async_computation | async-start | bytes 278528 | tf_op jit(solution)/shard_map/all_to_all | solution.py:98
  301.3 10.9 %all-to-all-start.1 = ((bf16[8,2,3456]{2,1,0:T(2,128)(2,1)}), bf16[8,2,3456]{2,1,0:T(2,128)(2,1)}, u32[]{:S(2)}, u32[]{:S(2)}) async-start(bf16[8,2,3456]{2,1,0:T(2,128)(2,1)} %reshape.1590), calls=%async_computation.1 | async-start | bytes 221184 | tf_op jit(solution)/shard_map/all_to_all | solution.py:102
  363.4 10.5 %all-to-all-start.2 = ((bf16[8,2,3456]{2,1,0:T(2,128)(2,1)}), bf16[8,2,3456]{2,1,0:T(2,128)(2,1)}, u32[]{:S(2)}, u32[]{:S(2)}) async-start(bf16[8,2,3456]{2,1,0:T(2,128)(2,1)} %reshape.1592), calls=%async_computation.2 | async-start | bytes 221184 | tf_op jit(solution)/shard_map/all_to_all | solution.py:98
  (75 other events, 199.0 us)
where the time goes:
time: 432 us; the launch traced here: 426 us
  other arithmetic  142 us (33%)
  local copies, waits for them, and re-layouts  140 us (32%)
  matrix products  41.5 us (10%)
  blocking collectives  32.7 us (8%)
  loops' own time  31.1 us (7%)
  starting transfers between devices  26.3 us (6%)
  waiting for transfers between devices  11.3 us (3%)
    while x45, other arithmetic  62.3 us
    eq x48, other arithmetic, advance(): degree == order_i  31.6 us
    another operation x1, loops' own time, legendre_table(): lax.scan(advance, (zero_rows, zero_rows), jnp.arange(amount, dtype=jnp.in...  31.1 us
    dot_general x18, matrix products, conv_taps(): jnp.dot(window, weight[row_tap, col_tap], preferred_element_type=jnp.floa...  29.2 us
    reshape x18, local copies, waits for them, and re-layouts, conv_taps(): padded[row_tap:row_tap + row_count, col_tap:col_tap + col_count]  29.2 us
    unnamed x41, local copies, waits for them, and re-layouts  26.1 us
    mul x8, local copies, waits for them, and re-layouts, per_device(): return grid_state + jax.nn.gelu(physical.astype(f32), approximate=False)  17.1 us
    sqrt x27, other arithmetic, advance(): jnp.sqrt(jnp.maximum(prior * prior - order_f * order_f, 0.0) / jnp.maximu...  13.6 us
  transfers between devices with their start and end apart: 11, of which 4 were waited for; matrix products, arithmetic and copies ran while one was open for 35% of the time, Pallas kernels for 0%

commit v1 on v0

--- a/solution.py
+++ b/solution.py
@@ -99,7 +99,10 @@
 
 
 def to_channels(values):
-    return lax.all_to_all(values, "lon", split_axis=0, concat_axis=2, tiled=True)
+    return jnp.concatenate(
+        lax.all_to_all(jnp.stack(jnp.split(values, lax.axis_size("lon"), axis=0)), "lon", 0, 0),
+        axis=2,
+    )
 
 
 def grid_rims(normed):

time: 432 us -> 478 us (1.11)
  local copies, waits for them, and re-layouts: 140 us -> 200 us
  matrix products: 41.5 us -> 25.8 us
    another operation x0 -> x18, local copies, waits for them, and re-layouts: none -> 27.8 us  [to_channels(): jnp.stack(jnp.split(values, lax.axis_size('lon'), axis=0))]
    unnamed x41 -> x77, local copies, waits for them, and re-layouts: 26.1 us -> 51.1 us
    slice x0 -> x15, local copies, waits for them, and re-layouts: none -> 19.5 us  [the longest x12 17.5 us: conv_taps(): padded[row_tap:row_tap + row_count, col_tap:col_tap + col_count]]
    dot_general x18, matrix products: 29.2 us -> 14.8 us  [conv_taps(): jnp.dot(window, weight[row_tap, col_tap], preferred_element_type=jnp.floa...]
    mul x8 -> x4, local copies, waits for them, and re-layouts: 17.1 us -> 7.97 us  [per_device(): return grid_state + jax.nn.gelu(physical.astype(f32), approximate=False)]
    all_to_all x3 -> x0, local copies, waits for them, and re-layouts: 5.84 us -> none  [to_channels(): lax.all_to_all(values, 'lon', split_axis=0, concat_axis=2, tiled=True)]
  transfers between devices with their start and end apart: 11 -> 11, of which waited for: 4 -> 6; matrix products, arithmetic and copies ran while one was open for 35% -> 31% of each run, Pallas kernels for 0% -> 0%
where the time goes in v1:
time: 478 us; the launch traced here: 471 us
  local copies, waits for them, and re-layouts  200 us (42%)
  other arithmetic  140 us (29%)
  blocking collectives  32.8 us (7%)
  loops' own time  31.8 us (7%)
  starting transfers between devices  26.8 us (6%)
  matrix products  25.8 us (5%)
  waiting for transfers between devices  12.9 us (3%)
    while x45, other arithmetic  62.2 us
    unnamed x77, local copies, waits for them, and re-layouts  51.1 us
    eq x48, other arithmetic, advance(): degree == order_i  32.3 us
    another operation x1, loops' own time, legendre_table(): lax.scan(advance, (zero_rows, zero_rows), jnp.arange(amount, dtype=jnp.in...  31.8 us
    reshape x18, local copies, waits for them, and re-layouts, conv_taps(): padded[row_tap:row_tap + row_count, col_tap:col_tap + col_count]  29.1 us
    another operation x18, local copies, waits for them, and re-layouts, to_channels(): jnp.stack(jnp.split(values, lax.axis_size('lon'), axis=0))  27.8 us
    slice x12, local copies, waits for them, and re-layouts, conv_taps(): padded[row_tap:row_tap + row_count, col_tap:col_tap + col_count]  17.5 us
    dot_general x18, matrix products, conv_taps(): jnp.dot(window, weight[row_tap, col_tap], preferred_element_type=jnp.floa...  14.8 us
  transfers between devices with their start and end apart: 11, of which 6 were waited for; matrix products, arithmetic and copies ran while one was open for 31% of the time, Pallas kernels for 0%

profile of v1, /device:TPU:0, one launch (start us, length us, event | category | flops | bytes accessed | tf_op | source)
XLA Modules:
  0.0 470.6 jit_solution(1066870435012493100)
XLA Ops:
  4.9 3.0 collective-permute-start
  10.1 153.6 %while.21 = (s32[]{:T(128)}, f32[6,48]{1,0:T(8,128)}, f32[6,48]{1,0:T(8,128)}, f32[3,16,6,48]{3,2,1,0:T(8,128)}, s32[3,16]{1,0:T(4,128)}, /*index=5*/s32[]{:T(12...) while((s32[]{:T(128)}, f32[6,48]{1,0:T(8,128)}, ...), condition=%wide.region_3.4_spmd.clone.clone.clone.clone, body=%wide.region_2.3_spmd.clone.clone.clone.clone.sunk | while | flops 65138 | bytes 363896 | solution.py:64
  163.7 5.6 %slice_bitcast_fusion = (bf16[3,3,384,384]{3,2,1,0:T(8,128)(2,1)}, bf16[3,3,384,384]{3,2,1,0:T(8,128)(2,1)}) fusion(bf16[2,3,3,384,384]{4,3,2,1,0:T(8,128)(2,1)} %param.9), kind=kLoop, calls=%fused_computation.125 | loop fusion | bytes 10616832 | tf_op jit(solution)/shard_map/squeeze | solution.py:144
  176.2 3.5 collective-permute-start.3
  231.2 3.5 collective-permute-start.7
  242.1 3.0 pad_maximum_fusion
  276.1 2.5 convert_bitcast_fusion
  278.6 2.9 copy.389
  281.5 3.5 reshape.1616
  284.9 4.5 all-to-all-start
  296.4 3.5 reshape.1617
  299.9 3.4 copy.390
  333.2 4.4 all-to-all-start.1
  338.4 5.8 %all-to-all-done.1 = bf16[8,2,3456]{2,1,0:T(2,128)(2,1)} async-done(((bf16[8,2,3456]{2,1,0:T(2,128)(2,1)}), bf16[8,2,3456]{2,1,0:T(2,128)(2,1)}, u32[]{:S(2)}, u32[]{:S(2)}) %all-to-all-start.1) | async-done | bytes 110624 | tf_op jit(solution)/shard_map/all_to_all | solution.py:103
  353.3 11.6 %all_gather.6 = bf16[48,6,768]{2,1,0:T(8,128)(2,1)S(1)} all-gather(bf16[12,6,768]{2,1,0:T(8,128)(2,1)} %reshape.1606), channel_id=1, replica_groups=mesh['lat'=4,'lon'=8] {'lat'}, dimensions={0}, use_global_device_ids=true | all-gather | bytes 552960 | tf_op jit(solution)/shard_map/all_gather | solution.py:168
  374.5 10.4 %all_gather.7 = bf16[48,6,768]{2,1,0:T(8,128)(2,1)S(1)} all-gather(bf16[12,6,768]{2,1,0:T(8,128)(2,1)S(1)} %multiply_convert_fusion), channel_id=1, replica_groups=mesh['lat'=4,'lon'=8] {'lat'}, dimensions={0}, use_global_device_ids=true | all-gather | bytes 552960 | tf_op jit(solution)/shard_map/all_gather | solution.py:176
  389.3 2.8 copy.401
  392.1 3.4 reshape.1620
  395.5 4.0 all-to-all-start.2
  402.2 3.7 all-to-all-done.2
  406.0 3.4 reshape.1621
  409.4 3.3 copy.402
  445.2 10.8 %all_to_all.40 = bf16[8,2,4320]{2,1,0:T(2,128)(2,1)} all-to-all(bf16[8,2,4320]{2,1,0:T(2,128)(2,1)} %reshape.1622), channel_id=1, replica_groups=mesh['lat'=4,'lon'=8] {'lon'}, dimensions={0} | all-to-all | bytes 276480 | tf_op jit(solution)/shard_map/all_to_all | solution.py:103
  468.2 2.5 fusion.65
  (536 shorter events, 333.3 us)
Async XLA Ops:
  0.0 369.4 %copy-start = (bf16[12,384,384]{2,1,0:T(8,128)(2,1)S(1)}, bf16[12,384,384]{2,1,0:T(8,128)(2,1)}, u32[]{:S(2)}) copy-start(bf16[12,384,384]{2,1,0:T(8,128)(2,1)} %param.10) | copy-start | bytes 10616836
  4.9 164.4 %collective-permute-start = (bf16[1,15,384]{2,1,0:T(8,128)(2,1)}, bf16[1,15,384]{2,1,0:T(8,128)(2,1)}, u32[]{:S(2)}, u32[]{:S(2)}) collective-permute-start(bf16[1,15,384]{2,1,0:T(8,128)(2,1)} %get-tuple-element.574), channel_id=1, source_target_pairs={{0,8},{8,16},{16,24},{24,0},{1,9},{9,17},{17,25},{25,1},{2,10},{10... | collective-permute-start | bytes 34568 | tf_op jit(solution)/shard_map/ppermute | solution.py:17
  7.8 161.4 %collective-permute-start.1 = (bf16[1,15,384]{2,1,0:T(8,128)(2,1)}, bf16[1,15,384]{2,1,0:T(8,128)(2,1)}, u32[]{:S(2)}, u32[]{:S(2)}) collective-permute-start(bf16[1,15,384]{2,1,0:T(8,128)(2,1)} %get-tuple-element.575), channel_id=1, source_target_pairs={{8,0},{16,8},{24,16},{0,24},{9,1},{17,9},{25,17},{1,25},{10,2},{18... | collective-permute-start | bytes 34568 | tf_op jit(solution)/shard_map/ppermute | solution.py:18
  35.2 6.6 %copy-start.33 = (f32[6]{0:T(128)}, f32[6]{0:T(128)S(1)}, u32[]{:S(2)}) copy-start(f32[6]{0:T(128)S(1)} %get-tuple-element.787) | copy-start | bytes 76 | tf_op jit(solution)/shard_map/while
  86.4 6.6 %copy-start.33 = (f32[6]{0:T(128)}, f32[6]{0:T(128)S(1)}, u32[]{:S(2)}) copy-start(f32[6]{0:T(128)S(1)} %get-tuple-element.787) | copy-start | bytes 76 | tf_op jit(solution)/shard_map/while
  94.4 4.6 copy-start.8
  137.6 6.6 %copy-start.33 = (f32[6]{0:T(128)}, f32[6]{0:T(128)S(1)}, u32[]{:S(2)}) copy-start(f32[6]{0:T(128)S(1)} %get-tuple-element.787) | copy-start | bytes 76 | tf_op jit(solution)/shard_map/while
  145.6 4.6 copy-start.8
  172.2 7.6 %collective-permute-start.2 = (bf16[14,1,384]{2,0,1:T(8,128)(2,1)}, bf16[14,1,384]{2,0,1:T(8,128)(2,1)S(1)}, u32[]{:S(2)}, u32[]{:S(2)}) collective-permute-start(bf16[14,1,384]{2,0,1:T(8,128)(2,1)} %copy.426), channel_id=1, source_target_pairs={{0,1},{1,2},{2,3},{3,4},{4,5},{5,6},{6,7},{7,0},{8,9},{9,10},{10,1... | collective-permute-start | bytes 32264 | tf_op jit(solution)/shard_map/ppermute | solution.py:17
  176.2 4.9 %collective-permute-start.3 = (bf16[14,1,384]{2,0,1:T(8,128)(2,1)S(1)}, bf16[14,1,384]{2,0,1:T(8,128)(2,1)S(1)}, u32[]{:S(2)}, u32[]{:S(2)}) collective-permute-start(bf16[14,1,384]{2,0,1:T(8,128)(2,1)S(1)} %copy.427), channel_id=1, source_target_pairs={{1,0},{2,1},{3,2},{4,3},{5,4},{6,5},{7,6},{0,7},{9,8},{10,9},{11,1... | collective-permute-start | bytes 32264 | tf_op jit(solution)/shard_map/ppermute | solution.py:18
  207.3 5.3 %copy-start.13 = (bf16[180,384]{1,0:T(8,128)(2,1)S(1)}, bf16[180,384]{1,0:T(8,128)(2,1)}, u32[]{:S(2)}) copy-start(bf16[180,384]{1,0:T(8,128)(2,1)} %reshape.1585) | copy-start | bytes 414724
  207.3 5.6 %copy-start.16 = (bf16[180,384]{1,0:T(8,128)(2,1)S(1)}, bf16[180,384]{1,0:T(8,128)(2,1)}, u32[]{:S(2)}) copy-start(bf16[180,384]{1,0:T(8,128)(2,1)} %reshape.1586) | copy-start | bytes 414724
  213.2 7.6 %copy-start.46 = (f32[384]{0:T(512)S(1)}, f32[384]{0:T(512)}, u32[]{:S(2)}) copy-start(f32[384]{0:T(512)} %get-tuple-element.402) | copy-start | bytes 4612
  221.0 5.3 %copy-start.6 = (bf16[12,15,384]{2,1,0:T(8,128)(2,1)}, bf16[12,15,384]{2,1,0:T(8,128)(2,1)S(1)}, u32[]{:S(2)}) copy-start(bf16[12,15,384]{2,1,0:T(8,128)(2,1)S(1)} %multiply_convert_fusion.1) | copy-start | bytes 414724
  221.0 4.6 collective-permute-start.4
  222.1 4.2 collective-permute-start.5
  228.3 6.5 %collective-permute-start.6 = (bf16[14,1,384]{2,0,1:T(8,128)(2,1)}, bf16[14,1,384]{2,0,1:T(8,128)(2,1)}, u32[]{:S(2)}, u32[]{:S(2)}) collective-permute-start(bf16[14,1,384]{2,0,1:T(8,128)(2,1)} %copy.374), channel_id=1, source_target_pairs={{0,1},{1,2},{2,3},{3,4},{4,5},{5,6},{6,7},{7,0},{8,9},{9,10},{10,1... | collective-permute-start | bytes 32264 | tf_op jit(solution)/shard_map/ppermute | solution.py:17
  231.2 5.2 %collective-permute-start.7 = (bf16[14,1,384]{2,0,1:T(8,128)(2,1)S(1)}, bf16[14,1,384]{2,0,1:T(8,128)(2,1)S(1)}, u32[]{:S(2)}, u32[]{:S(2)}) collective-permute-start(bf16[14,1,384]{2,0,1:T(8,128)(2,1)S(1)} %copy.375), channel_id=1, source_target_pairs={{1,0},{2,1},{3,2},{4,3},{5,4},{6,5},{7,6},{0,7},{9,8},{10,9},{11,1... | collective-permute-start | bytes 32264 | tf_op jit(solution)/shard_map/ppermute | solution.py:18
  265.1 5.3 %copy-start.14 = (bf16[180,384]{1,0:T(8,128)(2,1)S(1)}, bf16[180,384]{1,0:T(8,128)(2,1)}, u32[]{:S(2)}) copy-start(bf16[180,384]{1,0:T(8,128)(2,1)} %reshape.1594) | copy-start | bytes 414724
  265.1 5.6 %copy-start.15 = (bf16[180,384]{1,0:T(8,128)(2,1)S(1)}, bf16[180,384]{1,0:T(8,128)(2,1)}, u32[]{:S(2)}) copy-start(bf16[180,384]{1,0:T(8,128)(2,1)} %reshape.1595) | copy-start | bytes 414724
  276.1 17.7 %copy-start.47 = (s32[12,6]{0,1:T(8,128)S(1)}, s32[12,6]{0,1:T(8,128)}, u32[]{:S(2)}) copy-start(s32[12,6]{0,1:T(8,128)} %param.11) | copy-start | bytes 868
  284.9 11.5 %all-to-all-start = ((bf16[8,2,4320]{2,1,0:T(2,128)(2,1)}), bf16[8,2,4320]{2,1,0:T(2,128)(2,1)}, u32[]{:S(2)}, u32[]{:S(2)}) async-start(bf16[8,2,4320]{2,1,0:T(2,128)(2,1)} %reshape.1616), calls=%async_computation | async-start | bytes 278528 | tf_op jit(solution)/shard_map/all_to_all | solution.py:98
  333.2 10.9 %all-to-all-start.1 = ((bf16[8,2,3456]{2,1,0:T(2,128)(2,1)}), bf16[8,2,3456]{2,1,0:T(2,128)(2,1)}, u32[]{:S(2)}, u32[]{:S(2)}) async-start(bf16[8,2,3456]{2,1,0:T(2,128)(2,1)} %reshape.1618), calls=%async_computation.1 | async-start | bytes 221184 | tf_op jit(solution)/shard_map/all_to_all | solution.py:103
  395.5 10.5 %all-to-all-start.2 = ((bf16[8,2,3456]{2,1,0:T(2,128)(2,1)}), bf16[8,2,3456]{2,1,0:T(2,128)(2,1)}, u32[]{:S(2)}, u32[]{:S(2)}) async-start(bf16[8,2,3456]{2,1,0:T(2,128)(2,1)} %reshape.1620), calls=%async_computation.2 | async-start | bytes 221184 | tf_op jit(solution)/shard_map/all_to_all | solution.py:98
  (83 other events, 224.6 us)
